TPU v7x, 32 devices: a whole 2x2x4 slice. The times are simulated.
32 devices in a mesh: grp: 2 (over y), tok: 16 (over z, x, core).
Axes of the slice: x: 2, y: 2, z: 4, core: 2. Of those that a mesh axis runs over, the one named last changes fastest.
Arguments:
- hidden: bfloat16 [4, 1024, 1536], P('grp', 'tok'), parts along dimension 0
- base_ids: int32 [4, 1024], P('grp', 'tok'), parts along dimension 0, may hold values from 0 to 4, as said below
- attn_gain: bfloat16 [1536], replicated, may hold values from 0.099609375 to 1.8984375
- q_weight: bfloat16 [1536, 768], replicated
- kv_weight: bfloat16 [1536, 384], replicated
- out_weight: bfloat16 [768, 1536], replicated, may hold values from -0.21875 to 0.21875
- head_gain: bfloat16 [1536], replicated, may hold values from 0.099609375 to 1.8984375
- head_weight: bfloat16 [1536, 1536], replicated, may hold values from -0.15625 to 0.15625
- head_bias: float32 [1536], replicated, may hold values from -1 to 1
- track_perm: int32 [1536], replicated, may hold values from 0 to 1535, each once
Outputs:
- combined: float32 [2048, 1536], P(('grp', 'tok')), parts along dimension 0
There are 2 independent parts, one for each index of `grp`. A program takes and returns all parts, laid end to end along the dimension named above; an argument that names none is the same for every part. Nothing has to cross between parts.
Inputs may be any that keep to these rules, and one draw needn't show every extreme that they name: `base_ids`: every eighth token of each strand, from token 0, has a base 0 to 3.
All inputs are finite; a program needn't handle non-finite values.
Results may differ from a plain program's by a relative error of at most 0.0058.
Values may be sent and summed in bfloat16 or wider, within the bound.
No kernel may reach another device: no remote copies, remote signals or barrier semaphores. Data moves between devices by JAX's collectives and lax.ppermute only.
A program may use at most 128 MiB of HBM per device.

v0:
```python
import math
import jax
import jax.numpy as jnp
from jax import lax
from jax.sharding import PartitionSpec as P


def swapped(value, axis, distance):
    mask = 2**distance
    pairs = [(source, source ^ mask) for source in range(lax.axis_size(axis))]
    return lax.ppermute(value, axis, pairs)


def normalize(rows, gain):
    widened = rows.astype(jnp.float32)
    return (
        widened
        * lax.rsqrt(jnp.mean(widened * widened, -1, keepdims=True) + 1e-06)
        * gain.astype(jnp.float32)
    )


def attend(running, queries, key_value, usable_flag):
    maxima, totals, accumulated = running
    width_head = queries.shape[2]
    key_rows = key_value[:, :, :width_head]
    value_rows = key_value[:, :, width_head:]
    scores = jnp.einsum("srd,skd->srk", queries, key_rows, preferred_element_type=jnp.float32) * (
        1.0 / math.sqrt(width_head)
    )
    usable = usable_flag[:, None, :] > 0
    scores = jnp.where(usable, scores, jnp.float32(-1e30))
    new_maxima = jnp.maximum(maxima, jnp.max(scores, -1))
    weight_exp = jnp.where(usable, jnp.exp(scores - new_maxima[:, :, None]), jnp.float32(0.0))
    totals = jnp.sum(weight_exp, -1)
    summed = jnp.einsum(
        "srk,skd->srd",
        weight_exp.astype(jnp.bfloat16),
        value_rows,
        preferred_element_type=jnp.float32,
    )
    accumulated = summed
    return (new_maxima, totals, accumulated)


def per_device(
    hidden,
    base_ids,
    attn_gain,
    q_weight,
    kv_weight,
    out_weight,
    head_gain,
    head_weight,
    head_bias,
    track_perm,
):
    tok_rows = hidden.shape[1]
    width_head = kv_weight.shape[1] // 2
    head_count = q_weight.shape[1] // width_head
    bit_count = lax.axis_size("tok").bit_length() - 1
    normed = normalize(hidden, attn_gain).astype(jnp.bfloat16)
    key_value = jnp.einsum(
        "std,de->ste", normed, kv_weight, preferred_element_type=jnp.float32
    ).astype(jnp.bfloat16)
    usable_flag = (base_ids != 4).astype(jnp.bfloat16)
    partner = hidden[1]
    for bit_number in range(bit_count):
        partner = swapped(partner, "tok", bit_number)
    partner = partner[::-1]
    query_source = jnp.stack([normed[0], normalize(partner, attn_gain).astype(jnp.bfloat16)])
    residual_base = jnp.stack([hidden[0], partner])
    queries = jnp.einsum(
        "std,de->ste", query_source, q_weight, preferred_element_type=jnp.float32
    ).astype(jnp.bfloat16)
    queries = queries.reshape(2, tok_rows * head_count, width_head)
    row_count = queries.shape[1]
    start_state = (
        jnp.full((2, row_count), -1e30, jnp.float32),
        jnp.zeros((2, row_count), jnp.float32),
        jnp.zeros((2, row_count, width_head), jnp.float32),
    )
    softmax_state = attend(
        start_state,
        queries,
        lax.all_gather(key_value, "tok", axis=1, tiled=True),
        lax.all_gather(usable_flag, "tok", axis=1, tiled=True),
    )
    maxima, totals, accumulated = softmax_state
    attended = (
        (accumulated / totals[:, :, None])
        .astype(jnp.bfloat16)
        .reshape(2, tok_rows, head_count * width_head)
    )
    residual_sum = residual_base.astype(jnp.float32) + jnp.einsum(
        "ste,ed->std", attended, out_weight, preferred_element_type=jnp.float32
    )
    normed_out = normalize(residual_sum, head_gain).astype(jnp.bfloat16)
    forward_logits = (
        jnp.dot(normed_out[0], head_weight, preferred_element_type=jnp.float32) + head_bias
    )
    reverse_logits = (
        jnp.dot(normed_out[1], head_weight[:, track_perm], preferred_element_type=jnp.float32)
        + head_bias[track_perm]
    )
    forward_pred = jax.nn.softplus(forward_logits).astype(jnp.bfloat16)
    reverse_pred = jax.nn.softplus(reverse_logits).astype(jnp.bfloat16)
    return 0.5 * (forward_pred.astype(jnp.float32) + reverse_pred.astype(jnp.float32))


def solution(mesh):
    placed = (P("grp", "tok", None), P("grp", "tok"), P(), P(), P(), P(), P(), P(), P(), P())
    return jax.shard_map(
        per_device, mesh=mesh, in_specs=placed, out_specs=P(("grp", "tok"), None), check_vma=False
    )
```

profile of v0, /device:TPU:0, one launch (start us, length us, event | category | flops | bytes accessed | tf_op | source)
XLA Modules:
  0.0 101.3 jit_solution(12420879725566651075)
XLA Ops:
  6.5 0.0 all-gather.3.cloned.1.call-start
  6.6 0.8 convert_element_type.55
  7.4 1.2 %fusion.25 = f32[2,64]{1,0:T(2,128)S(1)} fusion(bf16[2,64,1536]{2,1,0:T(8,128)(2,1)} %param.10), kind=kLoop, calls=%fused_computation.31 | loop fusion | flops 589696 | bytes 393728 | tf_op jit(solution)/shard_map/reduce_sum | solution.py:18
  8.6 1.2 %fusion.27 = bf16[2,64,1536]{2,1,0:T(8,128)(2,1)S(1)} fusion(bf16[2,64,1536]{2,1,0:T(8,128)(2,1)} %param.10, f32[1536]{0:T(1024)S(1)} %convert_element_type.55, f32[2,64]{1,0:T(2,128)S(1)} %add_rsqrt_fusion.1), kind=kLoop, calls=%fused_computation.33 | loop fusion | flops 786432 | bytes 793088 | tf_op jit(solution)/shard_map/convert_element_type | solution.py:62
  9.8 0.0 copy-start.3
  9.8 2.4 %fusion.13 = bf16[2,64,384]{2,1,0:T(8,128)(2,1)} fusion(bf16[2,64,1536]{2,1,0:T(8,128)(2,1)S(1)} %fusion.27, bf16[1536,384]{1,0:T(8,128)(2,1)} %param.14), kind=kOutput, calls=%fused_computation.20 | convolution fusion | flops 151044096 | bytes 1671168 | tf_op jit(solution)/shard_map/std,de->ste/dot_general | solution.py:63
  12.2 0.0 all-gather.3.cloned.1.call-update
  12.3 0.6 collective-permute-start
  12.8 1.1 %collective-permute-done = bf16[64,1536]{1,0:T(8,128)(2,1)S(1)} collective-permute-done((bf16[64,1536]{1,0:T(8,128)(2,1)S(1)}, bf16[64,1536]{1,0:T(8,128)(2,1)S(1)}, u32[]{:S(2)}, u32[]{:S(2)}) %collective-permute-start) | collective-permute-done | bytes 196640 | tf_op jit(solution)/shard_map/ppermute | solution.py:11
  13.9 2.8 %collective-permute-start.1 = (bf16[64,1536]{1,0:T(8,128)(2,1)S(1)}, bf16[64,1536]{1,0:T(8,128)(2,1)S(1)}, u32[]{:S(2)}, u32[]{:S(2)}) collective-permute-start(bf16[64,1536]{1,0:T(8,128)(2,1)S(1)} %collective-permute-done), channel_id=1, source_target_pairs={{0,2},{1,3},{2,0},{3,1},{4,6},{5,7},{6,4},{7,5},{8,10},{9,11},{10,... | collective-permute-start | bytes 589832 | tf_op jit(solution)/shard_map/ppermute | solution.py:11
  16.7 20.7 %all-gather = bf16[16,64,2]{1,2,0:T(2,128)(2,1)S(1)} all-gather(bf16[1,64,2]{1,2,0:T(2,128)(2,1)S(1)} %fusion.37), channel_id=1, replica_groups=mesh['grp'=2,'tok'=16] {'tok'}, dimensions={0}, use_global_device_ids=true | all-gather | bytes 4352 | tf_op jit(solution)/shard_map/all_gather | solution.py:87
  37.4 11.5 %collective-permute-done.2 = bf16[64,1536]{1,0:T(8,128)(2,1)} collective-permute-done((bf16[64,1536]{1,0:T(8,128)(2,1)S(1)}, bf16[64,1536]{1,0:T(8,128)(2,1)}, u32[]{:S(2)}, u32[]{:S(2)}) %collective-permute-start.2) | collective-permute-done | bytes 196640 | tf_op jit(solution)/shard_map/ppermute | solution.py:11
  48.9 0.0 copy-start.5
  48.9 6.7 %copy.26 = bf16[1536,1536]{0,1:T(8,128)(2,1)} copy(bf16[1536,1536]{1,0:T(8,128)(2,1)} %param.17) | data formatting | bytes 9437184 | tf_op args[7]
  55.7 0.1 reshape.64
  55.8 0.0 copy-start.1
  55.8 13.4 %gather_fusion = bf16[1536,1536]{1,0:T(8,128)(2,1)} fusion(bf16[1536,1536]{0,1:T(8,128)(2,1)} %copy.26, s32[2048]{0:T(1024)S(1)} %pad_clamp_fusion), kind=kCustom, calls=%fused_computation | custom fusion | bytes 9443328 | tf_op jit(solution)/shard_map/gather | solution.py:103
  69.2 8.4 %gather_fusion.1 = f32[1536]{0:T(1024)S(1)} fusion(f32[1536]{0:T(1024)S(1)} %copy-done.1, s32[2048]{0:T(1024)S(1)} %pad_clamp_fusion), kind=kCustom, calls=%fused_computation.1 | custom fusion | bytes 18432 | tf_op jit(solution)/shard_map/gather | solution.py:104
  77.6 0.3 rev.3
  77.9 0.1 fusion.28
  78.1 0.1 fusion.36
  78.2 2.2 %fusion.10 = bf16[2,64,768]{2,1,0:T(8,128)(2,1)S(1)} fusion(bf16[1536,768]{1,0:T(8,128)(2,1)} %param.13, bf16[1,64,1536]{2,1,0:T(8,128)(2,1)S(1)} %fusion.36, bf16[1,64,1536]{2,1,0:T(8,128)(2,1)S(1)} %slice-done), kind=kOutput, calls=%fused_computation.19 | convolution fusion | flops 302284800 | bytes 2949120 | tf_op jit(solution)/shard_map/std,de->ste/dot_general | solution.py:73
  80.4 1.0 reshape.41
  81.3 2.0 %fusion.4 = (f32[2,256]{1,0:T(2,128)S(1)}, f32[2,256,1024]{2,1,0:T(8,128)S(1)}) fusion(pred[2,1024]{1,0:T(4,128)(4,1)S(1)} %bitcast.40, bf16[2,256,192]{2,1,0:T(8,128)(2,1)} %reshape.41, bf16[2,1024,384]{2,1,0:T(8,128)(2,1)} %all-gather.3.cloned.1.call-done), kind=kOutput, calls=%fused_computation.10 | convolution fusion | flops 202898944 | bytes 3411968 | tf_op jit(solution)/shard_map/srd,skd->srk/dot_general | solution.py:28
  83.4 0.6 fusion.5
  84.0 1.2 %fusion.9 = bf16[2,256,192]{1,2,0:T(8,128)(2,1)S(1)} fusion(f32[2,256,1024]{2,1,0:T(8,128)S(1)} %get-tuple-element.8, bf16[2,1024,384]{2,1,0:T(8,128)(2,1)S(1)} %copy-done.6, f32[2,256]{1,0:T(2,128)S(1)} %broadcast_maximum_fusion, pred[2,1024]{1,0:T(4,128)(4,1)S(1)} %bitcast.42, f32[2,256]{1,0:T(2,128)S(1)} %fusion.5), kind=kOutput, calls=%fused_computation.18 | convolution fusion | flops 204144640 | bytes 3350528 | tf_op jit(solution)/shard_map/srk,skd->srd/dot_general | solution.py:36
  85.2 0.1 copy.25
  85.3 0.3 reshape.42
  85.6 0.6 multiply_reduce_fusion
  86.2 0.2 multiply_convert_fusion
  86.4 3.4 %fusion.31 = bf16[64,1536]{1,0:T(8,128)(2,1)S(1)} fusion(bf16[1536,1536]{1,0:T(8,128)(2,1)} %param.17, bf16[2,64,1536]{2,1,0:T(8,128)(2,1)S(1)} %multiply_convert_fusion, f32[1536]{0:T(1024)S(1)} %copy-done.1), kind=kOutput, calls=%fused_computation.42 | convolution fusion | flops 302776320 | bytes 5120000 | tf_op jit(solution)/shard_map/dot_general | solution.py:100
  89.8 4.7 %add_multiply_fusion = f32[64,1536]{1,0:T(8,128)} fusion(bf16[1536,1536]{1,0:T(8,128)(2,1)} %gather_fusion, bf16[64,1536]{1,0:T(8,128)(2,1)S(1)} %fusion.31, bf16[2,64,1536]{2,1,0:T(8,128)(2,1)S(1)} %multiply_convert_fusion, f32[1536]{0:T(1024)S(1)} %gather_fusion.1), kind=kOutput, calls=%fused_computation.48 | convolution fusion | flops 303169536 | bytes 5513216 | tf_op jit(solution)/shard_map/dot_general | solution.py:103
  (31 shorter events, 0.1 us)
Async XLA Ops:
  6.5 79.1 %copy-start = (bf16[768,1536]{1,0:T(8,128)(2,1)S(1)}, bf16[768,1536]{1,0:T(8,128)(2,1)}, u32[]{:S(2)}) copy-start(bf16[768,1536]{1,0:T(8,128)(2,1)} %param.15) | copy-start | bytes 7077892
  6.5 5.7 %copy-start.2 = (bf16[2,64,1536]{2,1,0:T(8,128)(2,1)S(1)}, bf16[2,64,1536]{2,1,0:T(8,128)(2,1)}, u32[]{:S(2)}) copy-start(bf16[2,64,1536]{2,1,0:T(8,128)(2,1)} %param.10) | copy-start | bytes 1179652
  6.5 10.2 %copy-start.7 = (s32[2,64]{1,0:T(2,128)S(1)}, s32[2,64]{1,0:T(2,128)}, u32[]{:S(2)}) copy-start(s32[2,64]{1,0:T(2,128)} %param.11) | copy-start | bytes 1540
  6.5 30.9 %copy-start.4 = (s32[1536]{0:T(1024)S(1)}, s32[1536]{0:T(1024)}, u32[]{:S(2)}) copy-start(s32[1536]{0:T(1024)} %param.19) | copy-start | bytes 18436
  6.5 74.8 %all-gather.3.cloned.1.call-start = ((), (), s32[]{:S(2)}) async-start(), calls=%async_computation | async-start | bytes 1671168 | tf_op jit(solution)/shard_map/all_gather | solution.py:86
  9.8 45.9 %copy-start.3 = (bf16[2,64,1536]{2,1,0:T(8,128)(2,1)}, bf16[2,64,1536]{2,1,0:T(8,128)(2,1)S(1)}, u32[]{:S(2)}) copy-start(bf16[2,64,1536]{2,1,0:T(8,128)(2,1)S(1)} %fusion.27) | copy-start | bytes 1179652
  12.3 1.6 %collective-permute-start = (bf16[64,1536]{1,0:T(8,128)(2,1)S(1)}, bf16[64,1536]{1,0:T(8,128)(2,1)S(1)}, u32[]{:S(2)}, u32[]{:S(2)}) collective-permute-start(bf16[64,1536]{1,0:T(8,128)(2,1)S(1)} %get-tuple-element.6), channel_id=1, source_target_pairs={{0,1},{1,0},{2,3},{3,2},{4,5},{5,4},{6,7},{7,6},{8,9},{9,8},{10,11... | collective-permute-start | bytes 589832 | tf_op jit(solution)/shard_map/ppermute | solution.py:11
  13.9 23.5 %collective-permute-start.1 = (bf16[64,1536]{1,0:T(8,128)(2,1)S(1)}, bf16[64,1536]{1,0:T(8,128)(2,1)S(1)}, u32[]{:S(2)}, u32[]{:S(2)}) collective-permute-start(bf16[64,1536]{1,0:T(8,128)(2,1)S(1)} %collective-permute-done), channel_id=1, source_target_pairs={{0,2},{1,3},{2,0},{3,1},{4,6},{5,7},{6,4},{7,5},{8,10},{9,11},{10,... | collective-permute-start | bytes 589832 | tf_op jit(solution)/shard_map/ppermute | solution.py:11
  37.4 11.5 %collective-permute-start.2 = (bf16[64,1536]{1,0:T(8,128)(2,1)S(1)}, bf16[64,1536]{1,0:T(8,128)(2,1)}, u32[]{:S(2)}, u32[]{:S(2)}) collective-permute-start(bf16[64,1536]{1,0:T(8,128)(2,1)S(1)} %collective-permute-done.1), channel_id=1, source_target_pairs={{0,4},{1,5},{2,6},{3,7},{4,0},{5,1},{6,2},{7,3},{8,12},{9,13},{10,... | collective-permute-start | bytes 589832 | tf_op jit(solution)/shard_map/ppermute | solution.py:11
  48.9 28.7 %collective-permute-start.3 = (bf16[64,1536]{1,0:T(8,128)(2,1)}, bf16[64,1536]{1,0:T(8,128)(2,1)S(1)}, u32[]{:S(2)}, u32[]{:S(2)}) collective-permute-start(bf16[64,1536]{1,0:T(8,128)(2,1)} %collective-permute-done.2), channel_id=1, source_target_pairs={{0,8},{1,9},{2,10},{3,11},{4,12},{5,13},{6,14},{7,15},{8,0},{9,1},... | collective-permute-start | bytes 589832 | tf_op jit(solution)/shard_map/ppermute | solution.py:11
  48.9 6.8 %copy-start.5 = (bf16[1536]{0:T(1024)(128)(2,1)S(1)}, bf16[1536]{0:T(1024)(128)(2,1)}, u32[]{:S(2)}) copy-start(bf16[1536]{0:T(1024)(128)(2,1)} %param.16) | copy-start | bytes 9220
  55.8 13.4 %copy-start.1 = (f32[1536]{0:T(1024)S(1)}, f32[1536]{0:T(1024)}, u32[]{:S(2)}) copy-start(f32[1536]{0:T(1024)} %param.18) | copy-start | bytes 18436
  69.2 9.0 %slice-start = ((bf16[2,64,1536]{2,1,0:T(8,128)(2,1)}), bf16[1,64,1536]{2,1,0:T(8,128)(2,1)S(1)}, s32[]{:S(2)}) async-start(bf16[2,64,1536]{2,1,0:T(8,128)(2,1)} %copy-done.3), calls=%async_computation.1 | async-start | bytes 393216 | tf_op jit(solution)/shard_map/slice | solution.py:71
  81.3 2.7 %copy-start.6 = (bf16[2,1024,384]{2,1,0:T(8,128)(2,1)S(1)}, bf16[2,1024,384]{2,1,0:T(8,128)(2,1)}, u32[]{:S(2)}) copy-start(bf16[2,1024,384]{2,1,0:T(8,128)(2,1)} %all-gather.3.cloned.1.call-done) | copy-start | bytes 4718596
Sparse Core Ops, SparseCore 0:
  12.3 45.7 all-gather.2
where the time goes:
time: 102 us; the launch traced here: 101 us
  local copies, waits for them, and re-layouts  30.3 us (30%)
  blocking collectives  20.7 us (20%)
  matrix products  16.5 us (16%)
  between operations  13.6 us (13%)
  waiting for transfers between devices  12.6 us (12%)
  other arithmetic  4.27 us (4%)
  starting transfers between devices  3.44 us (3%)
    all_gather x1, blocking collectives, per_device(): lax.all_gather(usable_flag, 'tok', axis=1, tiled=True)  20.7 us
    gather x1, local copies, waits for them, and re-layouts, per_device(): head_weight[:, track_perm]  13.4 us
    ppermute x4, waiting for transfers between devices, swapped(): return lax.ppermute(value, axis, pairs)  12.5 us
    gather x1, local copies, waits for them, and re-layouts, per_device(): head_bias[track_perm]  8.38 us
    unnamed x17, local copies, waits for them, and re-layouts  6.77 us
    dot_general x1, matrix products, per_device(): jnp.dot(normed_out[1], head_weight[:, track_perm], preferred_element_type...  4.69 us
    dot_general x1, matrix products, per_device(): jnp.dot(normed_out[0], head_weight, preferred_element_type=jnp.float32)  3.42 us
    ppermute x4, starting transfers between devices, swapped(): return lax.ppermute(value, axis, pairs)  3.41 us
  transfers between devices with their start and end apart: 5, of which 2 were waited for; matrix products, arithmetic and copies ran while one was open for 32% of the time, Pallas kernels for 0%

commit v1 on v0

--- a/solution.py
+++ b/solution.py
@@ -3,6 +3,28 @@
 import jax.numpy as jnp
 from jax import lax
 from jax.sharding import PartitionSpec as P
+
+
+def joined_along(parts, dim):
+    shape = list(parts.shape[1:])
+    shape[dim] *= parts.shape[0]
+    return jnp.moveaxis(parts, 0, dim).reshape(shape)
+
+
+def grow_blocks(value, axis):
+    size = lax.axis_size(axis)
+    blocks = value[None]
+    for level in range(size.bit_length() - 1):
+        bit = 1 << level
+        other = lax.ppermute(blocks, axis, [(i, i ^ bit) for i in range(size)])
+        both = jnp.stack([blocks, other])
+        upper = lax.axis_index(axis) >> level & 1
+        blocks = jnp.where(upper == 0, both, both[::-1]).reshape(-1, *value.shape)
+    return blocks
+
+
+def gather_by_bits(x, axis, dim):
+    return joined_along(grow_blocks(x, axis), dim)
 
 
 def swapped(value, axis, distance):
@@ -84,7 +106,7 @@
         start_state,
         queries,
         lax.all_gather(key_value, "tok", axis=1, tiled=True),
-        lax.all_gather(usable_flag, "tok", axis=1, tiled=True),
+        gather_by_bits(usable_flag, "tok", 1),
     )
     maxima, totals, accumulated = softmax_state
     attended = (

time: 102 us -> 92.8 us (0.910)
  blocking collectives: 20.7 us -> 0 us
  starting transfers between devices: 3.44 us -> 14.1 us
  other arithmetic: 4.27 us -> 6.19 us
    all_gather x1 -> x0, blocking collectives: 20.7 us -> none  [per_device(): lax.all_gather(usable_flag, 'tok', axis=1, tiled=True)]
    ppermute x0 -> x4, starting transfers between devices: none -> 7.76 us  [grow_blocks(): other = lax.ppermute(blocks, axis, [(i, i ^ bit) for i in range(size)])]
    ppermute x4, waiting for transfers between devices: 12.5 us -> 8.42 us  [swapped(): return lax.ppermute(value, axis, pairs)]
    ppermute x0 -> x4, waiting for transfers between devices: none -> 3.14 us  [grow_blocks(): other = lax.ppermute(blocks, axis, [(i, i ^ bit) for i in range(size)])]
    ppermute x4, starting transfers between devices: 3.41 us -> 6.32 us  [swapped(): return lax.ppermute(value, axis, pairs)]
    another operation x0 -> x6, other arithmetic: none -> 2.07 us  [grow_blocks(): both = jnp.stack([blocks, other])]
    unnamed x17 -> x15, local copies, waits for them, and re-layouts: 6.77 us -> 6.78 us
  transfers between devices with their start and end apart: 5 -> 9, of which waited for: 2 -> 4; matrix products, arithmetic and copies ran while one was open for 32% -> 42% of each run, Pallas kernels for 0% -> 0%
where the time goes in v1:
time: 92.8 us; the launch traced here: 92.2 us
  local copies, waits for them, and re-layouts  30.3 us (33%)
  matrix products  16.5 us (18%)
  starting transfers between devices  14.1 us (15%)
  between operations  13.6 us (15%)
  waiting for transfers between devices  11.6 us (12%)
  other arithmetic  6.19 us (7%)
    gather x1, local copies, waits for them, and re-layouts, per_device(): head_weight[:, track_perm]  13.3 us
    ppermute x4, waiting for transfers between devices, swapped(): return lax.ppermute(value, axis, pairs)  8.42 us
    gather x1, local copies, waits for them, and re-layouts, per_device(): head_bias[track_perm]  8.38 us
    ppermute x4, starting transfers between devices, grow_blocks(): other = lax.ppermute(blocks, axis, [(i, i ^ bit) for i in range(size)])  7.76 us
    unnamed x15, local copies, waits for them, and re-layouts  6.78 us
    ppermute x4, starting transfers between devices, swapped(): return lax.ppermute(value, axis, pairs)  6.32 us
    dot_general x1, matrix products, per_device(): jnp.dot(normed_out[1], head_weight[:, track_perm], preferred_element_type...  4.69 us
    dot_general x1, matrix products, per_device(): jnp.dot(normed_out[0], head_weight, preferred_element_type=jnp.float32)  3.42 us
  transfers between devices with their start and end apart: 9, of which 4 were waited for; matrix products, arithmetic and copies ran while one was open for 42% of the time, Pallas kernels for 0%

profile of v1, /device:TPU:0, one launch (start us, length us, event | category | flops | bytes accessed | tf_op | source)
XLA Modules:
  0.0 92.2 jit_solution(10134519444621234286)
XLA Ops:
  6.5 0.8 fusion.39
  7.4 0.5 collective-permute-start.4
  7.9 0.7 convert_element_type.55
  8.6 1.2 %fusion.25 = f32[2,64]{1,0:T(2,128)S(1)} fusion(bf16[2,64,1536]{2,1,0:T(8,128)(2,1)} %param.10), kind=kLoop, calls=%fused_computation.31 | loop fusion | flops 589696 | bytes 393728 | tf_op jit(solution)/shard_map/reduce_sum | solution.py:40
  9.7 1.2 %fusion.27 = bf16[2,64,1536]{2,1,0:T(8,128)(2,1)S(1)} fusion(bf16[2,64,1536]{2,1,0:T(8,128)(2,1)} %param.10, f32[1536]{0:T(1024)S(1)} %convert_element_type.55, f32[2,64]{1,0:T(2,128)S(1)} %add_rsqrt_fusion.1), kind=kLoop, calls=%fused_computation.33 | loop fusion | flops 786432 | bytes 793088 | tf_op jit(solution)/shard_map/convert_element_type | solution.py:84
  10.9 2.4 %fusion.13 = bf16[2,64,384]{2,1,0:T(8,128)(2,1)} fusion(bf16[2,64,1536]{2,1,0:T(8,128)(2,1)S(1)} %fusion.27, bf16[1536,384]{1,0:T(8,128)(2,1)} %param.14), kind=kOutput, calls=%fused_computation.20 | convolution fusion | flops 151044096 | bytes 1671168 | tf_op jit(solution)/shard_map/std,de->ste/dot_general | solution.py:85
  13.4 0.6 fusion.45
  13.9 2.5 %collective-permute-start.5 = (bf16[2,2,64]{2,1,0:T(2,128)(2,1)}, bf16[2,2,64]{2,1,0:T(2,128)(2,1)}, u32[]{:S(2)}, u32[]{:S(2)}) collective-permute-start(bf16[2,2,64]{2,1,0:T(2,128)(2,1)} %get-tuple-element.8), channel_id=1, source_target_pairs={{0,2},{1,3},{2,0},{3,1},{4,6},{5,7},{6,4},{7,5},{8,10},{9,11},{10,... | collective-permute-start | bytes 1544 | tf_op jit(solution)/shard_map/ppermute | solution.py:19
  16.5 0.3 collective-permute-start
  16.8 1.6 %collective-permute-done.5 = bf16[2,2,64]{2,1,0:T(2,128)(2,1)} collective-permute-done((bf16[2,2,64]{2,1,0:T(2,128)(2,1)}, bf16[2,2,64]{2,1,0:T(2,128)(2,1)}, u32[]{:S(2)}, u32[]{:S(2)}) %collective-permute-start.5) | collective-permute-done | bytes 544 | tf_op jit(solution)/shard_map/ppermute | solution.py:19
  18.3 0.6 pad_maximum_fusion.3
  19.0 2.2 %collective-permute-start.6 = (bf16[4,2,64]{2,1,0:T(2,128)(2,1)S(1)}, bf16[4,2,64]{2,1,0:T(2,128)(2,1)S(1)}, u32[]{:S(2)}, u32[]{:S(2)}) collective-permute-start(bf16[4,2,64]{2,1,0:T(2,128)(2,1)S(1)} %bitcast.57), channel_id=1, source_target_pairs={{0,4},{1,5},{2,6},{3,7},{4,0},{5,1},{6,2},{7,3},{8,12},{9,13},{10,... | collective-permute-start | bytes 3080 | tf_op jit(solution)/shard_map/ppermute | solution.py:19
  21.2 1.6 %collective-permute-done.6 = bf16[4,2,64]{2,1,0:T(2,128)(2,1)S(1)} collective-permute-done((bf16[4,2,64]{2,1,0:T(2,128)(2,1)S(1)}, bf16[4,2,64]{2,1,0:T(2,128)(2,1)S(1)}, u32[]{:S(2)}, u32[]{:S(2)}) %collective-permute-start.6) | collective-permute-done | bytes 1056 | tf_op jit(solution)/shard_map/ppermute | solution.py:19
  22.7 2.0 %collective-permute-start.1 = (bf16[64,1536]{1,0:T(8,128)(2,1)S(1)}, bf16[64,1536]{1,0:T(8,128)(2,1)S(1)}, u32[]{:S(2)}, u32[]{:S(2)}) collective-permute-start(bf16[64,1536]{1,0:T(8,128)(2,1)S(1)} %collective-permute-done), channel_id=1, source_target_pairs={{0,2},{1,3},{2,0},{3,1},{4,6},{5,7},{6,4},{7,5},{8,10},{9,11},{10,... | collective-permute-start | bytes 589832 | tf_op jit(solution)/shard_map/ppermute | solution.py:33
  24.7 2.6 %collective-permute-start.7 = (bf16[8,2,64]{2,1,0:T(2,128)(2,1)S(1)}, bf16[8,2,64]{2,1,0:T(2,128)(2,1)S(1)}, u32[]{:S(2)}, u32[]{:S(2)}) collective-permute-start(bf16[8,2,64]{2,1,0:T(2,128)(2,1)S(1)} %bitcast.55), channel_id=1, source_target_pairs={{0,8},{1,9},{2,10},{3,11},{4,12},{5,13},{6,14},{7,15},{8,0},{9,1},... | collective-permute-start | bytes 6152 | tf_op jit(solution)/shard_map/ppermute | solution.py:19
  27.3 2.2 %collective-permute-done.1 = bf16[64,1536]{1,0:T(8,128)(2,1)S(1)} collective-permute-done((bf16[64,1536]{1,0:T(8,128)(2,1)S(1)}, bf16[64,1536]{1,0:T(8,128)(2,1)S(1)}, u32[]{:S(2)}, u32[]{:S(2)}) %collective-permute-start.1) | collective-permute-done | bytes 196640 | tf_op jit(solution)/shard_map/ppermute | solution.py:33
  29.5 1.6 %collective-permute-start.2 = (bf16[64,1536]{1,0:T(8,128)(2,1)S(1)}, bf16[64,1536]{1,0:T(8,128)(2,1)}, u32[]{:S(2)}, u32[]{:S(2)}) collective-permute-start(bf16[64,1536]{1,0:T(8,128)(2,1)S(1)} %collective-permute-done.1), channel_id=1, source_target_pairs={{0,4},{1,5},{2,6},{3,7},{4,0},{5,1},{6,2},{7,3},{8,12},{9,13},{10,... | collective-permute-start | bytes 589832 | tf_op jit(solution)/shard_map/ppermute | solution.py:33
  31.1 6.8 %copy.21 = bf16[1536,1536]{0,1:T(8,128)(2,1)} copy(bf16[1536,1536]{1,0:T(8,128)(2,1)} %param.17) | data formatting | bytes 9437184 | tf_op args[7]
  37.9 13.3 %gather_fusion = bf16[1536,1536]{1,0:T(8,128)(2,1)} fusion(bf16[1536,1536]{0,1:T(8,128)(2,1)} %copy.21, s32[2048]{0:T(1024)S(1)} %pad_clamp_fusion), kind=kCustom, calls=%fused_computation | custom fusion | bytes 9443328 | tf_op jit(solution)/shard_map/gather | solution.py:125
  51.2 8.4 %gather_fusion.1 = f32[1536]{0:T(1024)S(1)} fusion(f32[1536]{0:T(1024)S(1)} %copy-done.1, s32[2048]{0:T(1024)S(1)} %pad_clamp_fusion), kind=kCustom, calls=%fused_computation.1 | custom fusion | bytes 18432 | tf_op jit(solution)/shard_map/gather | solution.py:126
  59.7 2.5 %collective-permute-start.3 = (bf16[64,1536]{1,0:T(8,128)(2,1)}, bf16[64,1536]{1,0:T(8,128)(2,1)S(1)}, u32[]{:S(2)}, u32[]{:S(2)}) collective-permute-start(bf16[64,1536]{1,0:T(8,128)(2,1)} %collective-permute-done.2), channel_id=1, source_target_pairs={{0,8},{1,9},{2,10},{3,11},{4,12},{5,13},{6,14},{7,15},{8,0},{9,1},... | collective-permute-start | bytes 589832 | tf_op jit(solution)/shard_map/ppermute | solution.py:33
  62.3 6.2 %collective-permute-done.3 = bf16[64,1536]{1,0:T(8,128)(2,1)S(1)} collective-permute-done((bf16[64,1536]{1,0:T(8,128)(2,1)}, bf16[64,1536]{1,0:T(8,128)(2,1)S(1)}, u32[]{:S(2)}, u32[]{:S(2)}) %collective-permute-start.3) | collective-permute-done | bytes 196640 | tf_op jit(solution)/shard_map/ppermute | solution.py:33
  68.5 0.3 rev.15
  69.1 2.2 %fusion.10 = bf16[2,64,768]{2,1,0:T(8,128)(2,1)S(1)} fusion(bf16[1536,768]{1,0:T(8,128)(2,1)} %param.13, bf16[1,64,1536]{2,1,0:T(8,128)(2,1)S(1)} %fusion.36, bf16[1,64,1536]{2,1,0:T(8,128)(2,1)S(1)} %slice-done), kind=kOutput, calls=%fused_computation.19 | convolution fusion | flops 302284800 | bytes 2949120 | tf_op jit(solution)/shard_map/std,de->ste/dot_general | solution.py:95
  71.3 1.0 %reshape.63 = bf16[2,256,192]{2,1,0:T(8,128)(2,1)} reshape(bf16[2,64,768]{2,1,0:T(8,128)(2,1)S(1)} %fusion.10) | data formatting | bytes 393216 | tf_op jit(solution)/shard_map/reshape | solution.py:98
  72.3 2.0 %fusion.4 = (f32[2,256]{1,0:T(2,128)S(1)}, f32[2,256,1024]{2,1,0:T(8,128)S(1)}) fusion(pred[2,1024]{1,0:T(4,128)(4,1)S(1)} %gt.24, bf16[2,256,192]{2,1,0:T(8,128)(2,1)} %reshape.63, bf16[2,1024,384]{2,1,0:T(8,128)(2,1)} %all-gather.2.cloned.1.call-done), kind=kOutput, calls=%fused_computation.10 | convolution fusion | flops 202898944 | bytes 3411968 | tf_op jit(solution)/shard_map/srd,skd->srk/dot_general | solution.py:50
  74.3 0.6 fusion.5
  74.9 1.2 %fusion.9 = bf16[2,256,192]{1,2,0:T(8,128)(2,1)S(1)} fusion(f32[2,256,1024]{2,1,0:T(8,128)S(1)} %get-tuple-element.12, bf16[2,1024,384]{2,1,0:T(8,128)(2,1)S(1)} %copy-done.6, f32[2,256]{1,0:T(2,128)S(1)} %broadcast_maximum_fusion, pred[2,1024]{1,0:T(4,128)(4,1)S(1)} %gt.24, f32[2,256]{1,0:T(2,128)S(1)} %fusion.5), kind=kOutput, calls=%fused_computation.18 | convolution fusion | flops 204144640 | bytes 3350528 | tf_op jit(solution)/shard_map/srk,skd->srd/dot_general | solution.py:58
  76.3 0.3 reshape.64
  76.5 0.6 multiply_reduce_fusion
  77.3 3.4 %fusion.31 = bf16[64,1536]{1,0:T(8,128)(2,1)S(1)} fusion(bf16[1536,1536]{1,0:T(8,128)(2,1)} %param.17, bf16[2,64,1536]{2,1,0:T(8,128)(2,1)S(1)} %multiply_convert_fusion, f32[1536]{0:T(1024)S(1)} %copy-done.1), kind=kOutput, calls=%fused_computation.42 | convolution fusion | flops 302776320 | bytes 5120000 | tf_op jit(solution)/shard_map/dot_general | solution.py:122
  80.7 4.7 %add_multiply_fusion = f32[64,1536]{1,0:T(8,128)} fusion(bf16[1536,1536]{1,0:T(8,128)(2,1)} %gather_fusion, bf16[64,1536]{1,0:T(8,128)(2,1)S(1)} %fusion.31, bf16[2,64,1536]{2,1,0:T(8,128)(2,1)S(1)} %multiply_convert_fusion, f32[1536]{0:T(1024)S(1)} %gather_fusion.1), kind=kOutput, calls=%fused_computation.48 | convolution fusion | flops 303169536 | bytes 5513216 | tf_op jit(solution)/shard_map/dot_general | solution.py:125
  (43 shorter events, 0.9 us)
Async XLA Ops:
  6.5 70.0 %copy-start = (bf16[768,1536]{1,0:T(8,128)(2,1)S(1)}, bf16[768,1536]{1,0:T(8,128)(2,1)}, u32[]{:S(2)}) copy-start(bf16[768,1536]{1,0:T(8,128)(2,1)} %param.15) | copy-start | bytes 7077892
  6.5 9.9 %copy-start.2 = (bf16[2,64,1536]{2,1,0:T(8,128)(2,1)S(1)}, bf16[2,64,1536]{2,1,0:T(8,128)(2,1)}, u32[]{:S(2)}) copy-start(bf16[2,64,1536]{2,1,0:T(8,128)(2,1)} %param.10) | copy-start | bytes 1179652
  6.5 14.6 %copy-start.4 = (s32[1536]{0:T(1024)S(1)}, s32[1536]{0:T(1024)}, u32[]{:S(2)}) copy-start(s32[1536]{0:T(1024)} %param.19) | copy-start | bytes 18436
  6.5 65.7 %all-gather.2.cloned.1.call-start = ((), (), s32[]{:S(2)}) async-start(), calls=%async_computation | async-start | bytes 1671168 | tf_op jit(solution)/shard_map/all_gather | solution.py:108
  7.4 6.0 %collective-permute-start.4 = (bf16[1,2,64]{2,1,0:T(2,128)(2,1)S(1)}, bf16[1,2,64]{2,1,0:T(2,128)(2,1)S(1)}, u32[]{:S(2)}, u32[]{:S(2)}) collective-permute-start(bf16[1,2,64]{2,1,0:T(2,128)(2,1)S(1)} %get-tuple-element.10), channel_id=1, source_target_pairs={{0,1},{1,0},{2,3},{3,2},{4,5},{5,4},{6,7},{7,6},{8,9},{9,8},{10,11... | collective-permute-start | bytes 776 | tf_op jit(solution)/shard_map/ppermute | solution.py:19
  10.9 27.0 %copy-start.3 = (bf16[2,64,1536]{2,1,0:T(8,128)(2,1)}, bf16[2,64,1536]{2,1,0:T(8,128)(2,1)S(1)}, u32[]{:S(2)}) copy-start(bf16[2,64,1536]{2,1,0:T(8,128)(2,1)S(1)} %fusion.27) | copy-start | bytes 1179652
  13.9 4.4 %collective-permute-start.5 = (bf16[2,2,64]{2,1,0:T(2,128)(2,1)}, bf16[2,2,64]{2,1,0:T(2,128)(2,1)}, u32[]{:S(2)}, u32[]{:S(2)}) collective-permute-start(bf16[2,2,64]{2,1,0:T(2,128)(2,1)} %get-tuple-element.8), channel_id=1, source_target_pairs={{0,2},{1,3},{2,0},{3,1},{4,6},{5,7},{6,4},{7,5},{8,10},{9,11},{10,... | collective-permute-start | bytes 1544 | tf_op jit(solution)/shard_map/ppermute | solution.py:19
  16.5 6.2 %collective-permute-start = (bf16[64,1536]{1,0:T(8,128)(2,1)S(1)}, bf16[64,1536]{1,0:T(8,128)(2,1)S(1)}, u32[]{:S(2)}, u32[]{:S(2)}) collective-permute-start(bf16[64,1536]{1,0:T(8,128)(2,1)S(1)} %get-tuple-element.6), channel_id=1, source_target_pairs={{0,1},{1,0},{2,3},{3,2},{4,5},{5,4},{6,7},{7,6},{8,9},{9,8},{10,11... | collective-permute-start | bytes 589832 | tf_op jit(solution)/shard_map/ppermute | solution.py:33
  19.0 3.7 %collective-permute-start.6 = (bf16[4,2,64]{2,1,0:T(2,128)(2,1)S(1)}, bf16[4,2,64]{2,1,0:T(2,128)(2,1)S(1)}, u32[]{:S(2)}, u32[]{:S(2)}) collective-permute-start(bf16[4,2,64]{2,1,0:T(2,128)(2,1)S(1)} %bitcast.57), channel_id=1, source_target_pairs={{0,4},{1,5},{2,6},{3,7},{4,0},{5,1},{6,2},{7,3},{8,12},{9,13},{10,... | collective-permute-start | bytes 3080 | tf_op jit(solution)/shard_map/ppermute | solution.py:19
  22.7 6.8 %collective-permute-start.1 = (bf16[64,1536]{1,0:T(8,128)(2,1)S(1)}, bf16[64,1536]{1,0:T(8,128)(2,1)S(1)}, u32[]{:S(2)}, u32[]{:S(2)}) collective-permute-start(bf16[64,1536]{1,0:T(8,128)(2,1)S(1)} %collective-permute-done), channel_id=1, source_target_pairs={{0,2},{1,3},{2,0},{3,1},{4,6},{5,7},{6,4},{7,5},{8,10},{9,11},{10,... | collective-permute-start | bytes 589832 | tf_op jit(solution)/shard_map/ppermute | solution.py:33
  24.7 34.9 %collective-permute-start.7 = (bf16[8,2,64]{2,1,0:T(2,128)(2,1)S(1)}, bf16[8,2,64]{2,1,0:T(2,128)(2,1)S(1)}, u32[]{:S(2)}, u32[]{:S(2)}) collective-permute-start(bf16[8,2,64]{2,1,0:T(2,128)(2,1)S(1)} %bitcast.55), channel_id=1, source_target_pairs={{0,8},{1,9},{2,10},{3,11},{4,12},{5,13},{6,14},{7,15},{8,0},{9,1},... | collective-permute-start | bytes 6152 | tf_op jit(solution)/shard_map/ppermute | solution.py:19
  29.5 30.1 %collective-permute-start.2 = (bf16[64,1536]{1,0:T(8,128)(2,1)S(1)}, bf16[64,1536]{1,0:T(8,128)(2,1)}, u32[]{:S(2)}, u32[]{:S(2)}) collective-permute-start(bf16[64,1536]{1,0:T(8,128)(2,1)S(1)} %collective-permute-done.1), channel_id=1, source_target_pairs={{0,4},{1,5},{2,6},{3,7},{4,0},{5,1},{6,2},{7,3},{8,12},{9,13},{10,... | collective-permute-start | bytes 589832 | tf_op jit(solution)/shard_map/ppermute | solution.py:33
  31.1 6.8 %copy-start.5 = (bf16[1536]{0:T(1024)(128)(2,1)S(1)}, bf16[1536]{0:T(1024)(128)(2,1)}, u32[]{:S(2)}) copy-start(bf16[1536]{0:T(1024)(128)(2,1)} %param.16) | copy-start | bytes 9220
  37.9 13.3 %copy-start.1 = (f32[1536]{0:T(1024)S(1)}, f32[1536]{0:T(1024)}, u32[]{:S(2)}) copy-start(f32[1536]{0:T(1024)} %param.18) | copy-start | bytes 18436
  51.2 17.9 %slice-start = ((bf16[2,64,1536]{2,1,0:T(8,128)(2,1)}), bf16[1,64,1536]{2,1,0:T(8,128)(2,1)S(1)}, s32[]{:S(2)}) async-start(bf16[2,64,1536]{2,1,0:T(8,128)(2,1)} %copy-done.3), calls=%async_computation.1 | async-start | bytes 393216 | tf_op jit(solution)/shard_map/slice | solution.py:93
  59.7 8.8 %collective-permute-start.3 = (bf16[64,1536]{1,0:T(8,128)(2,1)}, bf16[64,1536]{1,0:T(8,128)(2,1)S(1)}, u32[]{:S(2)}, u32[]{:S(2)}) collective-permute-start(bf16[64,1536]{1,0:T(8,128)(2,1)} %collective-permute-done.2), channel_id=1, source_target_pairs={{0,8},{1,9},{2,10},{3,11},{4,12},{5,13},{6,14},{7,15},{8,0},{9,1},... | collective-permute-start | bytes 589832 | tf_op jit(solution)/shard_map/ppermute | solution.py:33
  72.3 2.7 %copy-start.6 = (bf16[2,1024,384]{2,1,0:T(8,128)(2,1)S(1)}, bf16[2,1024,384]{2,1,0:T(8,128)(2,1)}, u32[]{:S(2)}) copy-start(bf16[2,1024,384]{2,1,0:T(8,128)(2,1)} %all-gather.2.cloned.1.call-done) | copy-start | bytes 4718596
Sparse Core Ops, SparseCore 0:
  13.5 42.6 all-gather.1
